TPU v7x, 32 devices: a whole 2x2x4 slice. The times are simulated.
32 devices in a mesh: groups: 2 (over x), loop: 16 (over z, y, core).
Axes of the slice: x: 2, y: 2, z: 4, core: 2. Of those that a mesh axis runs over, the one named last changes fastest.
Arguments:
- queries: bfloat16 [16384, 2048], P(('groups', 'loop')), parts along dimension 0, may hold values from -16 to 16, as said below
- key_rows: bfloat16 [16384, 2048], P(('groups', 'loop')), parts along dimension 0, may hold values from -12 to 12, as said below
- values: bfloat16 [16384, 2048], P(('groups', 'loop')), parts along dimension 0, may hold values from -24 to 24
Outputs:
- attended: bfloat16 [16384, 2048], P(('groups', 'loop')), parts along dimension 0
- profile: float32 [4096], P('groups'), parts along dimension 0
There are 2 independent parts, one for each index of `groups`. A program takes and returns all parts, laid end to end along the dimension named above; each array names one. Nothing has to cross between parts.
Inputs may be any that keep to these rules, and one draw needn't show every extreme that they name: Real-valued queries. `key_rows`: Real-valued keys of order one.
All inputs are finite; a program needn't handle non-finite values.
Results may differ from a plain program's by a relative error of at most 0.0049.
Values may be sent and summed in bfloat16 or wider, within the bound.
A program may use at most 128 MiB of HBM per device.

v0:
```python
import math

import jax
import jax.numpy as jnp
from jax import lax
from jax.sharding import PartitionSpec as P

HEADS = 16
HEAD_DIM = 128
WINDOW = 2048


def passed_along(value, axis, steps):
    count = lax.axis_size(axis)
    pairs = [(source, (source + steps) % count) for source in range(count)]
    return lax.ppermute(value, axis, pairs)


def attend(query_block, key_ext, value_ext):
    row_count = query_block.shape[0]
    ext_count = key_ext.shape[0]
    scale = HEAD_DIM ** (-0.5)
    query_pos = lax.broadcasted_iota(jnp.int32, (row_count, ext_count), 0)
    key_pos = lax.broadcasted_iota(jnp.int32, (row_count, ext_count), 1)
    allowed = (key_pos > query_pos) & (key_pos <= query_pos + WINDOW)

    def one_head(head_index, output_buf):
        column = head_index * HEAD_DIM
        q_head = lax.dynamic_slice_in_dim(query_block, column, HEAD_DIM, 1)
        k_head = lax.dynamic_slice_in_dim(key_ext, column, HEAD_DIM, 1)
        v_head = lax.dynamic_slice_in_dim(value_ext, column, HEAD_DIM, 1)
        scores = (
            lax.dot_general(
                q_head, k_head, (((1,), (1,)), ((), ())), preferred_element_type=jnp.float32
            )
            * scale
        )
        scores = jnp.where(allowed, scores, jnp.float32(-1e30))
        top = jnp.max(scores, axis=1, keepdims=True)
        expo = jnp.exp(scores - top)
        weights = (expo / jnp.sum(expo, axis=1, keepdims=True)).astype(jnp.bfloat16)
        head_out = jnp.dot(weights, v_head, preferred_element_type=jnp.float32).astype(jnp.bfloat16)
        return lax.dynamic_update_slice_in_dim(output_buf, head_out, column, 1)

    return lax.fori_loop(0, HEADS, one_head, jnp.zeros(query_block.shape, jnp.bfloat16))


def body(queries, key_rows, values):
    row_count = queries.shape[0]
    reach_count = WINDOW // row_count
    near_keys, near_values = passed_along((key_rows, values), "loop", 1)
    for level in range(reach_count.bit_length() - 1):
        far_keys, far_values = passed_along((near_keys, near_values), "loop", 1 << level)
        near_keys = jnp.concatenate([far_keys, near_keys], axis=0)
        near_values = jnp.concatenate([far_values, near_values], axis=0)
    key_ext = jnp.concatenate([near_keys, key_rows], axis=0)
    value_ext = jnp.concatenate([near_values, values], axis=0)
    attended = attend(queries, key_ext, value_ext)
    local_sum = jnp.sum(attended.astype(jnp.float32), axis=0)
    total = lax.psum(local_sum, "loop")
    profile = total / math.sqrt(row_count * lax.axis_size("loop"))
    return (attended, profile)


def solution(mesh):
    return jax.shard_map(
        body,
        mesh=mesh,
        in_specs=(
            P(("groups", "loop"), None),
            P(("groups", "loop"), None),
            P(("groups", "loop"), None),
        ),
        out_specs=(P(("groups", "loop"), None), P("groups")),
        check_vma=False,
    )
```

profile of v0, /device:TPU:0, one launch (start us, length us, event | category | flops | bytes accessed | tf_op | source)
XLA Modules:
  0.0 416.9 jit_solution(2512011049518232460)
XLA Ops:
  3.8 26.3 %collective-permute-done.3 = bf16[512,2048]{1,0:T(8,128)(2,1)S(1)} collective-permute-done((bf16[512,2048]{1,0:T(8,128)(2,1)}, bf16[512,2048]{1,0:T(8,128)(2,1)S(1)}, u32[]{:S(2)}, u32[]{:S(2)}) %collective-permute-start.3) | collective-permute-done | bytes 2097184 | tf_op jit(solution)/shard_map/ppermute | solution.py:16
  30.1 22.5 %collective-permute-done = bf16[512,2048]{1,0:T(8,128)(2,1)S(1)} collective-permute-done((bf16[512,2048]{1,0:T(8,128)(2,1)}, bf16[512,2048]{1,0:T(8,128)(2,1)S(1)}, u32[]{:S(2)}, u32[]{:S(2)}) %collective-permute-start) | collective-permute-done | bytes 2097184 | tf_op jit(solution)/shard_map/ppermute | solution.py:16
  52.5 22.5 %collective-permute-done.4 = bf16[512,2048]{1,0:T(8,128)(2,1)S(1)} collective-permute-done((bf16[512,2048]{1,0:T(8,128)(2,1)S(1)}, bf16[512,2048]{1,0:T(8,128)(2,1)S(1)}, u32[]{:S(2)}, u32[]{:S(2)}) %collective-permute-start.4) | collective-permute-done | bytes 2097184 | tf_op jit(solution)/shard_map/ppermute | solution.py:16
  77.6 33.3 %collective-permute-done.1 = bf16[512,2048]{1,0:T(8,128)(2,1)S(1)} collective-permute-done((bf16[512,2048]{1,0:T(8,128)(2,1)S(1)}, bf16[512,2048]{1,0:T(8,128)(2,1)S(1)}, u32[]{:S(2)}, u32[]{:S(2)}) %collective-permute-start.1) | collective-permute-done | bytes 2097184 | tf_op jit(solution)/shard_map/ppermute | solution.py:16
  116.0 58.1 %collective-permute-done.5 = bf16[1024,2048]{1,0:T(8,128)(2,1)} collective-permute-done((bf16[1024,2048]{1,0:T(8,128)(2,1)}, bf16[1024,2048]{1,0:T(8,128)(2,1)}, u32[]{:S(2)}, u32[]{:S(2)}) %collective-permute-start.5) | collective-permute-done | bytes 4194336 | tf_op jit(solution)/shard_map/ppermute | solution.py:16
  174.1 10.2 %pad_maximum_fusion.1 = bf16[2560,2048]{1,0:T(8,128)(2,1)} fusion(bf16[512,2048]{1,0:T(8,128)(2,1)} %param.7, bf16[512,2048]{1,0:T(8,128)(2,1)} %copy-done, bf16[512,2048]{1,0:T(8,128)(2,1)} %copy-done.3, bf16[1024,2048]{1,0:T(8,128)(2,1)} %collective-permute-done.5), kind=kLoop, calls=%fused_computation.17 | loop fusion | flops 41943040 | bytes 20971520 | tf_op jit(solution)/shard_map/concatenate | solution.py:57
  184.3 79.7 %collective-permute-done.2 = bf16[1024,2048]{1,0:T(8,128)(2,1)} collective-permute-done((bf16[1024,2048]{1,0:T(8,128)(2,1)}, bf16[1024,2048]{1,0:T(8,128)(2,1)}, u32[]{:S(2)}, u32[]{:S(2)}) %collective-permute-start.2) | collective-permute-done | bytes 4194336 | tf_op jit(solution)/shard_map/ppermute | solution.py:16
  264.0 13.6 %pad_maximum_fusion = bf16[2560,2048]{1,0:T(8,128)(2,1)} fusion(bf16[512,2048]{1,0:T(8,128)(2,1)S(1)} %copy-done.5, bf16[512,2048]{1,0:T(8,128)(2,1)S(1)} %collective-permute-done, bf16[512,2048]{1,0:T(8,128)(2,1)S(1)} %copy-done.2, bf16[1024,2048]{1,0:T(8,128)(2,1)} %collective-permute-done.2), kind=kLoop, calls=%fused_computation.16 | loop fusion | flops 41943040 | bytes 20971520 | tf_op jit(solution)/shard_map/concatenate | solution.py:56
  277.8 93.0 %while.14 = (s32[]{:T(128)}, bf16[512,2048]{1,0:T(8,128)(2,1)S(1)}, bf16[512,2048]{1,0:T(8,128)(2,1)}, bf16[2560,2048]{1,0:T(8,128)(2,1)}, bf16[2560,2048]{1,0:T...) while((s32[]{:T(128)}, bf16[512,2048]{1,0:T(8,128)(2,1)S(1)}, ...), condition=%wide.region_3.4_spmd.clone, body=%wide.region_0.3_spmd.clone.sunk | while | flops 685571072 | bytes 17315988 | solution.py:45
  277.8 2.8 fusion.18
  283.6 2.8 fusion.18
  295.2 2.8 fusion.18
  301.0 2.8 fusion.18
  306.9 2.8 fusion.18
  312.7 2.8 fusion.18
  318.5 2.8 fusion.18
  324.3 2.8 fusion.18
  330.1 2.8 fusion.18
  335.9 2.8 fusion.18
  341.7 2.8 fusion.18
  347.5 2.8 fusion.18
  353.4 2.8 fusion.18
  359.2 2.8 fusion.18
  371.2 45.1 %psum.7 = f32[2048]{0:T(1024)S(1)} all-reduce(f32[2048]{0:T(1024)S(1)} %convert_reduce_fusion), channel_id=1, replica_groups=mesh['groups'=2,'loop'=16] {'loop'}, use_global_device_ids=true, to_apply=%region_5.6 | all-reduce | flops 2048 | bytes 16384 | tf_op jit(solution)/shard_map/psum | solution.py:60
  (58 shorter events, 65.3 us)
Async XLA Ops:
  0.6 29.4 %collective-permute-start.3 = (bf16[512,2048]{1,0:T(8,128)(2,1)}, bf16[512,2048]{1,0:T(8,128)(2,1)S(1)}, u32[]{:S(2)}, u32[]{:S(2)}) collective-permute-start(bf16[512,2048]{1,0:T(8,128)(2,1)} %param.7), channel_id=1, source_target_pairs={{0,1},{1,2},{2,3},{3,4},{4,5},{5,6},{6,7},{7,8},{8,9},{9,10},{10,1... | collective-permute-start | bytes 6291464 | tf_op jit(solution)/shard_map/ppermute | solution.py:16
  1.1 51.4 %collective-permute-start = (bf16[512,2048]{1,0:T(8,128)(2,1)}, bf16[512,2048]{1,0:T(8,128)(2,1)S(1)}, u32[]{:S(2)}, u32[]{:S(2)}) collective-permute-start(bf16[512,2048]{1,0:T(8,128)(2,1)} %param.6), channel_id=1, source_target_pairs={{0,1},{1,2},{2,3},{3,4},{4,5},{5,6},{6,7},{7,8},{8,9},{9,10},{10,1... | collective-permute-start | bytes 6291464 | tf_op jit(solution)/shard_map/ppermute | solution.py:16
  30.1 84.7 %copy-start = (bf16[512,2048]{1,0:T(8,128)(2,1)}, bf16[512,2048]{1,0:T(8,128)(2,1)S(1)}, u32[]{:S(2)}) copy-start(bf16[512,2048]{1,0:T(8,128)(2,1)S(1)} %collective-permute-done.3) | copy-start | bytes 6291460
  30.1 44.9 %collective-permute-start.4 = (bf16[512,2048]{1,0:T(8,128)(2,1)S(1)}, bf16[512,2048]{1,0:T(8,128)(2,1)S(1)}, u32[]{:S(2)}, u32[]{:S(2)}) collective-permute-start(bf16[512,2048]{1,0:T(8,128)(2,1)S(1)} %collective-permute-done.3), channel_id=1, source_target_pairs={{0,1},{1,2},{2,3},{3,4},{4,5},{5,6},{6,7},{7,8},{8,9},{9,10},{10,1... | collective-permute-start | bytes 6291464 | tf_op jit(solution)/shard_map/ppermute | solution.py:16
  52.5 58.3 %collective-permute-start.1 = (bf16[512,2048]{1,0:T(8,128)(2,1)S(1)}, bf16[512,2048]{1,0:T(8,128)(2,1)S(1)}, u32[]{:S(2)}, u32[]{:S(2)}) collective-permute-start(bf16[512,2048]{1,0:T(8,128)(2,1)S(1)} %collective-permute-done), channel_id=1, source_target_pairs={{0,1},{1,2},{2,3},{3,4},{4,5},{5,6},{6,7},{7,8},{8,9},{9,10},{10,1... | collective-permute-start | bytes 6291464 | tf_op jit(solution)/shard_map/ppermute | solution.py:16
  75.0 39.8 %copy-start.3 = (bf16[512,2048]{1,0:T(8,128)(2,1)}, bf16[512,2048]{1,0:T(8,128)(2,1)S(1)}, u32[]{:S(2)}) copy-start(bf16[512,2048]{1,0:T(8,128)(2,1)S(1)} %collective-permute-done.4) | copy-start | bytes 6291460
  77.6 96.5 %collective-permute-start.5 = (bf16[1024,2048]{1,0:T(8,128)(2,1)}, bf16[1024,2048]{1,0:T(8,128)(2,1)}, u32[]{:S(2)}, u32[]{:S(2)}) collective-permute-start(bf16[1024,2048]{1,0:T(8,128)(2,1)} %pad_maximum_fusion.3), channel_id=1, source_target_pairs={{0,2},{1,3},{2,4},{3,5},{4,6},{5,7},{6,8},{7,9},{8,10},{9,11},{10,... | collective-permute-start | bytes 12582920 | tf_op jit(solution)/shard_map/ppermute | solution.py:16
  110.8 1.3 copy-start.1
  114.8 149.2 %collective-permute-start.2 = (bf16[1024,2048]{1,0:T(8,128)(2,1)}, bf16[1024,2048]{1,0:T(8,128)(2,1)}, u32[]{:S(2)}, u32[]{:S(2)}) collective-permute-start(bf16[1024,2048]{1,0:T(8,128)(2,1)} %pad_maximum_fusion.2), channel_id=1, source_target_pairs={{0,2},{1,3},{2,4},{3,5},{4,6},{5,7},{6,8},{7,9},{8,10},{9,11},{10,... | collective-permute-start | bytes 12582920 | tf_op jit(solution)/shard_map/ppermute | solution.py:16
  116.0 148.0 %copy-start.2 = (bf16[512,2048]{1,0:T(8,128)(2,1)S(1)}, bf16[512,2048]{1,0:T(8,128)(2,1)}, u32[]{:S(2)}) copy-start(bf16[512,2048]{1,0:T(8,128)(2,1)} %copy-done.1) | copy-start | bytes 6291460
  116.0 148.0 %copy-start.5 = (bf16[512,2048]{1,0:T(8,128)(2,1)S(1)}, bf16[512,2048]{1,0:T(8,128)(2,1)}, u32[]{:S(2)}) copy-start(bf16[512,2048]{1,0:T(8,128)(2,1)} %param.6) | copy-start | bytes 6291460
  370.8 46.1 %copy-start.4 = (bf16[512,2048]{1,0:T(8,128)(2,1)}, bf16[512,2048]{1,0:T(8,128)(2,1)S(1)}, u32[]{:S(2)}) copy-start(bf16[512,2048]{1,0:T(8,128)(2,1)S(1)} %get-tuple-element.109) | copy-start | bytes 6291460
where the time goes:
time: 418 us; the launch traced here: 417 us
  waiting for transfers between devices  242 us (58%)
  matrix products  79.1 us (19%)
  blocking collectives  45.1 us (11%)
  other arithmetic  43.5 us (10%)
  starting transfers between devices  4.36 us (1%)
    ppermute x6, waiting for transfers between devices, passed_along(): return lax.ppermute(value, axis, pairs)  242 us
    psum x1, blocking collectives, body(): total = lax.psum(local_sum, 'loop')  45.1 us
    dot_general x16, matrix products, one_head(): lax.dot_general(q_head, k_head, (((1,), (1,)), ((), ())), preferred_eleme...  45 us
    dot_general x16, matrix products, one_head(): jnp.dot(weights, v_head, preferred_element_type=jnp.float32)  34.1 us
    concatenate x1, other arithmetic, body(): key_ext = jnp.concatenate([near_keys, key_rows], axis=0)  13.6 us
    reduce_sum x16, other arithmetic, one_head(): weights = (expo / jnp.sum(expo, axis=1, keepdims=True)).astype(jnp.bfloat16)  13.5 us
    concatenate x1, other arithmetic, body(): value_ext = jnp.concatenate([near_values, values], axis=0)  10.2 us
  transfers between devices with their start and end apart: 6, of which 6 were waited for; matrix products, arithmetic and copies ran while one was open for 4% of the time, Pallas kernels for 0%

commit v1 on v0

v1 whole, which is shorter than its diff:
```python
import functools
import math

import jax
import jax.numpy as jnp
from jax import lax
from jax.experimental import pallas as pl
from jax.experimental.pallas import tpu as pltpu
from jax.sharding import PartitionSpec as P

HEADS = 16
HEAD_DIM = 128
WINDOW = 2048
MESH = pl.DeviceIdType.MESH
PLANE = 4
TILE = 256
AHEAD = 2
COEF = HEAD_DIM ** (-0.5) * math.log2(math.e)


def attend_tile(q, keys, vals):
    nt = (((1,), (1,)), ((), ()))
    s = lax.dot_general(q, keys, nt, preferred_element_type=jnp.float32)
    row = lax.broadcasted_iota(jnp.int32, (TILE, TILE), 0)
    col = lax.broadcasted_iota(jnp.int32, (TILE, TILE), 1)
    upper = col > row
    edge = jnp.where(upper, s[:, :TILE], s[:, WINDOW:])
    mid = s[:, TILE:WINDOW]
    top = jnp.maximum(
        jnp.max(mid, axis=1, keepdims=True), jnp.max(edge, axis=1, keepdims=True)
    )
    p_mid = jnp.exp2((mid - top) * COEF)
    p_edge = jnp.exp2((edge - top) * COEF)
    total = jnp.sum(p_mid, axis=1, keepdims=True) + jnp.sum(p_edge, axis=1, keepdims=True)
    p_first = jnp.where(upper, p_edge, 0.0).astype(jnp.bfloat16)
    p_last = jnp.where(upper, 0.0, p_edge).astype(jnp.bfloat16)
    p = jnp.concatenate([p_first, p_mid.astype(jnp.bfloat16), p_last], axis=1)
    out = jnp.dot(p, vals, preferred_element_type=jnp.float32)
    return (out / total).astype(jnp.bfloat16)


def kernel(
    n, q_ref, k_ref, v_ref, o_ref, prof_ref,
    q_buf, kv, sums, planes,
    q_sem, own_sem, z_send, y_send, c_send, recv, sum_send, sum_recv,
):
    rows = q_ref.shape[0]
    me = lax.axis_index("loop")
    a, b = me // PLANE, me % PLANE
    y, c = b // 2, b % 2
    y_peer = me + 2 - 4 * y
    c_peer = me + 1 - 2 * c
    z_peer = lax.rem(me + PLANE, n)
    base = me - b
    plane_count = n // PLANE

    def block(h, slot):
        return kv.at[h, :, pl.ds(pl.multiple_of(slot * rows, rows), rows), :]

    def own_copies(h):
        cols = pl.ds(pl.multiple_of(h * HEAD_DIM, HEAD_DIM), HEAD_DIM)
        mine = pl.ds(PLANE * rows, rows)
        return (
            pltpu.make_async_copy(k_ref.at[:, cols], kv.at[h, 0, mine, :], own_sem.at[0, h]),
            pltpu.make_async_copy(v_ref.at[:, cols], kv.at[h, 1, mine, :], own_sem.at[1, h]),
        )

    def send(h, src, dst, send_sem, peer):
        return pltpu.make_async_remote_copy(
            src_ref=block(h, src),
            dst_ref=block(h, dst),
            send_sem=send_sem,
            recv_sem=recv.at[dst, h],
            device_id={"loop": peer},
            device_id_type=MESH,
        )

    def z_copy(h):
        return send(h, PLANE, 0, z_send.at[h], z_peer)

    def y_copy(h):
        return send(h, jnp.where(y == 0, PLANE, 0), 2, y_send.at[h], y_peer)

    def c_near(h):
        return send(h, jnp.where(c == 0, PLANE, 2), 3, c_send.at[0, h], c_peer)

    def c_far(h):
        return send(h, jnp.where(c == 0, 2, 0), 1, c_send.at[1, h], c_peer)

    q_copy = pltpu.make_async_copy(q_ref, q_buf, q_sem)

    def load(h, carry):
        for copy in own_copies(h):
            copy.start()
        return carry

    lax.fori_loop(0, HEADS, load, 0)
    q_copy.start()

    barrier = pltpu.get_barrier_semaphore()
    for k in range(1, PLANE):
        pl.semaphore_signal(
            barrier, inc=1, device_id={"loop": base + lax.rem(b + k, PLANE)}, device_id_type=MESH
        )
    for k in range(1, plane_count):
        pl.semaphore_signal(
            barrier, inc=1, device_id={"loop": lax.rem(me + PLANE * k, n)}, device_id_type=MESH
        )
    pl.semaphore_wait(barrier, PLANE - 1 + plane_count - 1)

    for h in range(AHEAD):
        for copy in own_copies(h):
            copy.wait()
        z_copy(h).start()
    q_copy.wait()

    def compute(h):
        cols = pl.ds(pl.multiple_of(h * HEAD_DIM, HEAD_DIM), HEAD_DIM)
        partial = jnp.zeros((1, HEAD_DIM), jnp.float32)
        for tile in range(rows // TILE):
            at = pl.ds(tile * TILE, TILE)
            span = pl.ds(tile * TILE, TILE + WINDOW)
            out = attend_tile(q_buf[at, cols], kv[h, 0, span, :], kv[h, 1, span, :])
            o_ref[at, cols] = out
            partial += jnp.sum(out.astype(jnp.float32), axis=0, keepdims=True)
        sums[b, pl.ds(h, 1), :] = partial

    def step(t, carry):
        @pl.when(t < HEADS)
        def _():
            z_copy(t).wait_recv()
            y_copy(t).start()
            z_copy(t).wait_send()

            @pl.when(t + AHEAD < HEADS)
            def _():
                for copy in own_copies(t + AHEAD):
                    copy.wait()
                z_copy(t + AHEAD).start()

        @pl.when((t >= 1) & (t <= HEADS))
        def _():
            y_copy(t - 1).wait_recv()
            c_near(t - 1).start()
            c_far(t - 1).start()

        @pl.when(t >= 2)
        def _():
            c_near(t - 2).wait_recv()
            c_far(t - 2).wait_recv()
            compute(t - 2)

        return carry

    lax.fori_loop(0, HEADS + 2, step, 0)

    def exchange(buf, slot, peer, stage, index):
        return pltpu.make_async_remote_copy(
            src_ref=buf.at[slot],
            dst_ref=buf.at[slot],
            send_sem=sum_send.at[stage, index],
            recv_sem=sum_recv.at[stage, index],
            device_id={"loop": peer},
            device_id_type=MESH,
        )

    copies = [
        exchange(sums, b, base + lax.rem(b + k, PLANE), 0, k) for k in range(1, PLANE)
    ]
    for copy in copies:
        copy.start()

    def drain(h, carry):
        y_copy(h).wait_send()
        c_near(h).wait_send()
        c_far(h).wait_send()
        return carry

    lax.fori_loop(0, HEADS, drain, 0)
    for k, copy in enumerate(copies, 1):
        copy.wait_send()
        exchange(sums, lax.rem(b + PLANE - k, PLANE), me, 0, k).wait_recv()
    plane = sums[0]
    for k in range(1, PLANE):
        plane += sums[k]
    planes[a] = plane
    copies = [
        exchange(planes, a, lax.rem(me + PLANE * k, n), 1, k) for k in range(1, plane_count)
    ]
    for copy in copies:
        copy.start()
    for k, copy in enumerate(copies, 1):
        copy.wait_send()
        exchange(planes, lax.rem(a + plane_count - k, plane_count), me, 1, k).wait_recv()
    total = planes[0]
    for k in range(1, plane_count):
        total += planes[k]
    prof_ref[...] = total / math.sqrt(rows * n)


def body(n, queries, key_rows, values):
    rows, width = queries.shape
    plane_count = n // PLANE
    if rows * PLANE != WINDOW or n % PLANE or plane_count < 2:
        raise ValueError("unsupported sizes")
    stages = max(PLANE, plane_count)
    any_spec = pl.BlockSpec(memory_space=pl.ANY)
    vmem_spec = pl.BlockSpec(memory_space=pltpu.VMEM)
    dma = pltpu.SemaphoreType.DMA
    attended, profile = pl.pallas_call(
        functools.partial(kernel, n),
        out_shape=(
            jax.ShapeDtypeStruct((rows, width), jnp.bfloat16),
            jax.ShapeDtypeStruct((HEADS, HEAD_DIM), jnp.float32),
        ),
        in_specs=[any_spec] * 3,
        out_specs=(vmem_spec, vmem_spec),
        scratch_shapes=[
            pltpu.VMEM((rows, width), jnp.bfloat16),
            pltpu.VMEM((HEADS, 2, (PLANE + 1) * rows, HEAD_DIM), jnp.bfloat16),
            pltpu.VMEM((PLANE, HEADS, HEAD_DIM), jnp.float32),
            pltpu.VMEM((plane_count, HEADS, HEAD_DIM), jnp.float32),
            dma,
            dma((2, HEADS)),
            dma((HEADS,)),
            dma((HEADS,)),
            dma((2, HEADS)),
            dma((PLANE, HEADS)),
            dma((2, stages)),
            dma((2, stages)),
        ],
        compiler_params=pltpu.CompilerParams(
            collective_id=0, has_side_effects=True, vmem_limit_bytes=56 * 1024 * 1024
        ),
        name="ring_attention",
    )(queries, key_rows, values)
    return attended, profile.reshape(width)


def solution(mesh):
    n = mesh.shape["loop"]
    return jax.shard_map(
        lambda q, k, v: body(n, q, k, v),
        mesh=mesh,
        in_specs=(
            P(("groups", "loop"), None),
            P(("groups", "loop"), None),
            P(("groups", "loop"), None),
        ),
        out_specs=(P(("groups", "loop"), None), P("groups")),
        check_vma=False,
    )
```

time: 418 us -> 121 us (0.29)
  waiting for transfers between devices: 242 us -> 0 us
  Pallas kernels: 0 us -> 117 us
  matrix products: 79.1 us -> 0 us
  blocking collectives: 45.1 us -> 0 us
  other arithmetic: 43.5 us -> 0 us
  starting transfers between devices: 4.36 us -> 0 us
    ppermute x6 -> x0, waiting for transfers between devices: 242 us -> none  [passed_along(): return lax.ppermute(value, axis, pairs)]
    pallas_call x0 -> x1, Pallas kernels: none -> 117 us  [body(): pl.pallas_call(functools.partial(kernel, n), out_shape=(jax.ShapeDtypeStr...]
    dot_general x32 -> x0, matrix products: 79.1 us -> none  [the longest x16 45 us: one_head(): lax.dot_general(q_head, k_head, (((1,), (1,)), ((), ())), preferred_eleme...]
    psum x1 -> x0, blocking collectives: 45.1 us -> none  [body(): total = lax.psum(local_sum, 'loop')]
    concatenate x4 -> x0, other arithmetic: 28.9 us -> none  [the longest x1 13.6 us: body(): key_ext = jnp.concatenate([near_keys, key_rows], axis=0)]
    reduce_sum x17 -> x0, other arithmetic: 13.9 us -> none  [the longest x16 13.5 us: one_head(): weights = (expo / jnp.sum(expo, axis=1, keepdims=True)).astype(jnp.bfloat16)]
    ppermute x6 -> x0, starting transfers between devices: 4.36 us -> none  [passed_along(): return lax.ppermute(value, axis, pairs)]
  transfers between devices with their start and end apart: 6 -> 0, of which waited for: 6 -> 0; matrix products, arithmetic and copies ran while one was open for 4% -> 0% of each run, Pallas kernels for 0% -> 0%
where the time goes in v1:
time: 121 us
  Pallas kernels  117 us (97%)
  local copies, waits for them, and re-layouts  3.77 us (3%)
    pallas_call x1, Pallas kernels, body(): pl.pallas_call(functools.partial(kernel, n), out_shape=(jax.ShapeDtypeStr...  117 us
    unnamed x4, local copies, waits for them, and re-layouts  3.77 us

profile of v1, /device:TPU:0, one launch (start us, length us, event | category | flops | bytes accessed | tf_op | source)
XLA Modules:
  0.0 120.9 jit_solution(7405463768910674644)
XLA Ops:
  0.6 116.5 %ring_attention.1 = (bf16[512,2048]{1,0:T(8,128)(2,1)}, f32[16,128]{1,0:T(8,128)}) custom-call(bf16[512,2048]{1,0:T(8,128)(2,1)} %q_ref.1, bf16[512,2048]{1,0:T(8,128)(2,1)} %k_ref.1, bf16[512,2048]{1,0:T(8,128)(2,1)} %v_ref.1), custom_call_target="tpu_custom_call" | custom-call | tf_op jit(solution)/shard_map/ring_attention/pallas_call | solution.py:210
  117.2 0.0 copy-start
  117.2 3.2 %copy.7 = bf16[512,2048]{1,0:T(8,128)(2,1)} copy(bf16[512,2048]{1,0:T(8,128)(2,1)} %get-tuple-element.8) | data formatting | bytes 4194304
  120.3 0.0 copy-done
  120.3 0.6 copy.8
Async XLA Ops:
  117.2 3.2 %copy-start = (f32[16,128]{1,0:T(8,128)S(1)}, f32[16,128]{1,0:T(8,128)}, u32[]{:S(2)}) copy-start(f32[16,128]{1,0:T(8,128)} %get-tuple-element.5) | copy-start | bytes 24580

commit v2 on v1

--- a/solution.py
+++ b/solution.py
@@ -14,11 +14,15 @@
 MESH = pl.DeviceIdType.MESH
 PLANE = 4
 TILE = 256
-AHEAD = 2
+SPLIT = 1
+LAG_Y = 2
+LAG_C = 1
+LOADED = 4
+AHEAD = 4
 COEF = HEAD_DIM ** (-0.5) * math.log2(math.e)
 
 
-def attend_tile(q, keys, vals):
+def weigh_tile(q, keys):
     nt = (((1,), (1,)), ((), ()))
     s = lax.dot_general(q, keys, nt, preferred_element_type=jnp.float32)
     row = lax.broadcasted_iota(jnp.int32, (TILE, TILE), 0)
@@ -35,13 +39,12 @@
     p_first = jnp.where(upper, p_edge, 0.0).astype(jnp.bfloat16)
     p_last = jnp.where(upper, 0.0, p_edge).astype(jnp.bfloat16)
     p = jnp.concatenate([p_first, p_mid.astype(jnp.bfloat16), p_last], axis=1)
-    out = jnp.dot(p, vals, preferred_element_type=jnp.float32)
-    return (out / total).astype(jnp.bfloat16)
+    return p, 1.0 / total
 
 
 def kernel(
     n, q_ref, k_ref, v_ref, o_ref, prof_ref,
-    q_buf, kv, sums, planes,
+    q_buf, kv, p_buf, inv, sums, planes,
     q_sem, own_sem, z_send, y_send, c_send, recv, sum_send, sum_recv,
 ):
     rows = q_ref.shape[0]
@@ -54,23 +57,37 @@
     base = me - b
     plane_count = n // PLANE
 
-    def block(h, slot):
-        return kv.at[h, :, pl.ds(pl.multiple_of(slot * rows, rows), rows), :]
-
-    def own_copies(h):
-        cols = pl.ds(pl.multiple_of(h * HEAD_DIM, HEAD_DIM), HEAD_DIM)
+    part = rows // SPLIT
+    pieces = 2 * HEADS * SPLIT
+
+    def block(p, slot):
+        at = pl.multiple_of(slot * rows + lax.rem(p, SPLIT) * part, part)
+        return kv.at[p // SPLIT, pl.ds(at, part), :]
+
+    def own_start(r):
+        cols = pl.ds(pl.multiple_of((r // 2) * HEAD_DIM, HEAD_DIM), HEAD_DIM)
+        mine = kv.at[r, pl.ds(PLANE * rows, rows), :]
+
+        @pl.when(lax.rem(r, 2) == 0)
+        def _():
+            pltpu.make_async_copy(k_ref.at[:, cols], mine, own_sem.at[r]).start()
+
+        @pl.when(lax.rem(r, 2) == 1)
+        def _():
+            pltpu.make_async_copy(v_ref.at[:, cols], mine, own_sem.at[r]).start()
+
+    def own_wait(p):
         mine = pl.ds(PLANE * rows, rows)
-        return (
-            pltpu.make_async_copy(k_ref.at[:, cols], kv.at[h, 0, mine, :], own_sem.at[0, h]),
-            pltpu.make_async_copy(v_ref.at[:, cols], kv.at[h, 1, mine, :], own_sem.at[1, h]),
-        )
-
-    def send(h, src, dst, send_sem, peer):
+        pltpu.make_async_copy(
+            k_ref.at[:, pl.ds(0, HEAD_DIM)], kv.at[p // SPLIT, mine, :], own_sem.at[p // SPLIT]
+        ).wait()
+
+    def send(p, src, dst, send_sem, peer):
         return pltpu.make_async_remote_copy(
-            src_ref=block(h, src),
-            dst_ref=block(h, dst),
+            src_ref=block(p, src),
+            dst_ref=block(p, dst),
             send_sem=send_sem,
-            recv_sem=recv.at[dst, h],
+            recv_sem=recv.at[dst, p],
             device_id={"loop": peer},
             device_id_type=MESH,
         )
@@ -89,13 +106,12 @@
 
     q_copy = pltpu.make_async_copy(q_ref, q_buf, q_sem)
 
-    def load(h, carry):
-        for copy in own_copies(h):
-            copy.start()
+    def load(r, carry):
+        own_start(r)
         return carry
 
-    lax.fori_loop(0, HEADS, load, 0)
-    q_copy.start()
+    for r in range(LOADED):
+        own_start(jnp.int32(r))
 
     barrier = pltpu.get_barrier_semaphore()
     for k in range(1, PLANE):
@@ -108,51 +124,75 @@
         )
     pl.semaphore_wait(barrier, PLANE - 1 + plane_count - 1)
 
-    for h in range(AHEAD):
-        for copy in own_copies(h):
-            copy.wait()
-        z_copy(h).start()
+    for p in range(AHEAD):
+        if p % SPLIT == 0:
+            own_wait(p)
+        z_copy(p).start()
+    q_copy.start()
+    lax.fori_loop(LOADED, 2 * HEADS, load, 0)
     q_copy.wait()
 
-    def compute(h):
+    def weigh(h, tile):
+        cols = pl.ds(pl.multiple_of(h * HEAD_DIM, HEAD_DIM), HEAD_DIM)
+        p, scale = weigh_tile(
+            q_buf[pl.ds(tile * TILE, TILE), cols],
+            kv[2 * h, pl.ds(tile * TILE, TILE + WINDOW), :],
+        )
+        p_buf[tile] = p
+        inv[tile] = scale
+
+    def gather(h):
         cols = pl.ds(pl.multiple_of(h * HEAD_DIM, HEAD_DIM), HEAD_DIM)
         partial = jnp.zeros((1, HEAD_DIM), jnp.float32)
         for tile in range(rows // TILE):
-            at = pl.ds(tile * TILE, TILE)
-            span = pl.ds(tile * TILE, TILE + WINDOW)
-            out = attend_tile(q_buf[at, cols], kv[h, 0, span, :], kv[h, 1, span, :])
-            o_ref[at, cols] = out
+            vals = kv[2 * h + 1, pl.ds(tile * TILE, TILE + WINDOW), :]
+            out = jnp.dot(p_buf[tile], vals, preferred_element_type=jnp.float32)
+            out = (out * inv[tile]).astype(jnp.bfloat16)
+            o_ref[pl.ds(tile * TILE, TILE), cols] = out
             partial += jnp.sum(out.astype(jnp.float32), axis=0, keepdims=True)
         sums[b, pl.ds(h, 1), :] = partial
 
     def step(t, carry):
-        @pl.when(t < HEADS)
+        @pl.when(t < pieces)
         def _():
             z_copy(t).wait_recv()
             y_copy(t).start()
             z_copy(t).wait_send()
 
-            @pl.when(t + AHEAD < HEADS)
+            @pl.when(t + AHEAD < pieces)
             def _():
-                for copy in own_copies(t + AHEAD):
-                    copy.wait()
+                @pl.when(lax.rem(t + AHEAD, SPLIT) == 0)
+                def _():
+                    own_wait(t + AHEAD)
+
                 z_copy(t + AHEAD).start()
 
-        @pl.when((t >= 1) & (t <= HEADS))
-        def _():
-            y_copy(t - 1).wait_recv()
-            c_near(t - 1).start()
-            c_far(t - 1).start()
-
-        @pl.when(t >= 2)
-        def _():
-            c_near(t - 2).wait_recv()
-            c_far(t - 2).wait_recv()
-            compute(t - 2)
+        @pl.when((t >= LAG_Y) & (t < pieces + LAG_Y))
+        def _():
+            y_copy(t - LAG_Y).wait_recv()
+            c_near(t - LAG_Y).start()
+            c_far(t - LAG_Y).start()
+
+        @pl.when(t >= LAG_Y + LAG_C)
+        def _():
+            u = t - LAG_Y - LAG_C
+            c_near(u).wait_recv()
+            c_far(u).wait_recv()
+            phase = lax.rem(u, 2 * SPLIT)
+            head = u // (2 * SPLIT)
+            for tile in range(rows // TILE):
+
+                @pl.when(phase == SPLIT - 1)
+                def _():
+                    weigh(head, tile)
+
+            @pl.when(phase == 2 * SPLIT - 1)
+            def _():
+                gather(head)
 
         return carry
 
-    lax.fori_loop(0, HEADS + 2, step, 0)
+    lax.fori_loop(0, pieces + LAG_Y + LAG_C, step, 0)
 
     def exchange(buf, slot, peer, stage, index):
         return pltpu.make_async_remote_copy(
@@ -176,7 +216,7 @@
         c_far(h).wait_send()
         return carry
 
-    lax.fori_loop(0, HEADS, drain, 0)
+    lax.fori_loop(0, pieces, drain, 0)
     for k, copy in enumerate(copies, 1):
         copy.wait_send()
         exchange(sums, lax.rem(b + PLANE - k, PLANE), me, 0, k).wait_recv()
@@ -203,8 +243,9 @@
     plane_count = n // PLANE
     if rows * PLANE != WINDOW or n % PLANE or plane_count < 2:
         raise ValueError("unsupported sizes")
+    pieces = 2 * HEADS * SPLIT
     stages = max(PLANE, plane_count)
-    any_spec = pl.BlockSpec(memory_space=pl.ANY)
+    hbm_spec = pl.BlockSpec(memory_space=pltpu.HBM)
     vmem_spec = pl.BlockSpec(memory_space=pltpu.VMEM)
     dma = pltpu.SemaphoreType.DMA
     attended, profile = pl.pallas_call(
@@ -213,24 +254,26 @@
             jax.ShapeDtypeStruct((rows, width), jnp.bfloat16),
             jax.ShapeDtypeStruct((HEADS, HEAD_DIM), jnp.float32),
         ),
-        in_specs=[any_spec] * 3,
+        in_specs=[hbm_spec] * 3,
         out_specs=(vmem_spec, vmem_spec),
         scratch_shapes=[
             pltpu.VMEM((rows, width), jnp.bfloat16),
-            pltpu.VMEM((HEADS, 2, (PLANE + 1) * rows, HEAD_DIM), jnp.bfloat16),
+            pltpu.VMEM((2 * HEADS, (PLANE + 1) * rows, HEAD_DIM), jnp.bfloat16),
+            pltpu.VMEM((rows // TILE, TILE, TILE + WINDOW), jnp.bfloat16),
+            pltpu.VMEM((rows // TILE, TILE, 1), jnp.float32),
             pltpu.VMEM((PLANE, HEADS, HEAD_DIM), jnp.float32),
             pltpu.VMEM((plane_count, HEADS, HEAD_DIM), jnp.float32),
             dma,
-            dma((2, HEADS)),
-            dma((HEADS,)),
-            dma((HEADS,)),
-            dma((2, HEADS)),
-            dma((PLANE, HEADS)),
+            dma((2 * HEADS,)),
+            dma((pieces,)),
+            dma((pieces,)),
+            dma((2, pieces)),
+            dma((PLANE, pieces)),
             dma((2, stages)),
             dma((2, stages)),
         ],
         compiler_params=pltpu.CompilerParams(
-            collective_id=0, has_side_effects=True, vmem_limit_bytes=56 * 1024 * 1024
+            collective_id=0, has_side_effects=True, vmem_limit_bytes=51 * 1024 * 1024
         ),
         name="ring_attention",
     )(queries, key_rows, values)

time: 121 us -> 115 us (0.950)
  Pallas kernels: 117 us -> 112 us
  local copies, waits for them, and re-layouts: 3.77 us -> 1.92 us
    pallas_call x1, Pallas kernels: 117 us -> 112 us  [body(): pl.pallas_call(functools.partial(kernel, n), out_shape=(jax.ShapeDtypeStr...]
    unnamed x4 -> x2, local copies, waits for them, and re-layouts: 3.77 us -> 1.92 us
where the time goes in v2:
time: 115 us
  Pallas kernels  112 us (97%)
  local copies, waits for them, and re-layouts  1.92 us (2%)
    pallas_call x1, Pallas kernels, body(): pl.pallas_call(functools.partial(kernel, n), out_shape=(jax.ShapeDtypeStr...  112 us

profile of v2, /device:TPU:0, one launch (start us, length us, event | category | flops | bytes accessed | tf_op | source)
XLA Modules:
  0.0 114.5 jit_solution(4357489772805291614)
XLA Ops:
  0.6 111.9 %ring_attention.1 = (bf16[512,2048]{1,0:T(8,128)(2,1)S(1)}, f32[16,128]{1,0:T(8,128)S(1)}) custom-call(bf16[512,2048]{1,0:T(8,128)(2,1)} %q_ref.1, bf16[512,2048]{1,0:T(8,128)(2,1)} %k_ref.1, bf16[512,2048]{1,0:T(8,128)(2,1)} %v_ref.1), custom_call_target="tpu_custom_call" | custom-call | tf_op jit(solution)/shard_map/ring_attention/pallas_call | solution.py:251
  112.6 1.3 %copy.7 = bf16[512,2048]{1,0:T(8,128)(2,1)} copy(bf16[512,2048]{1,0:T(8,128)(2,1)S(1)} %get-tuple-element.8) | data formatting | bytes 4194304
  113.9 0.6 copy.8

commit v3 on v2

--- a/solution.py
+++ b/solution.py
@@ -15,10 +15,10 @@
 PLANE = 4
 TILE = 256
 SPLIT = 1
-LAG_Y = 2
+LAG_Y = 3
 LAG_C = 1
-LOADED = 4
-AHEAD = 4
+LOADED = 6
+AHEAD = 6
 COEF = HEAD_DIM ** (-0.5) * math.log2(math.e)
 
 
@@ -44,7 +44,7 @@
 
 def kernel(
     n, q_ref, k_ref, v_ref, o_ref, prof_ref,
-    q_buf, kv, p_buf, inv, sums, planes,
+    q_buf, kv, p_buf, inv, sums, planes, lasts,
     q_sem, own_sem, z_send, y_send, c_send, recv, sum_send, sum_recv,
 ):
     rows = q_ref.shape[0]
@@ -114,15 +114,11 @@
         own_start(jnp.int32(r))
 
     barrier = pltpu.get_barrier_semaphore()
-    for k in range(1, PLANE):
+    for k in range(1, n):
         pl.semaphore_signal(
-            barrier, inc=1, device_id={"loop": base + lax.rem(b + k, PLANE)}, device_id_type=MESH
+            barrier, inc=1, device_id={"loop": lax.rem(me + k, n)}, device_id_type=MESH
         )
-    for k in range(1, plane_count):
-        pl.semaphore_signal(
-            barrier, inc=1, device_id={"loop": lax.rem(me + PLANE * k, n)}, device_id_type=MESH
-        )
-    pl.semaphore_wait(barrier, PLANE - 1 + plane_count - 1)
+    pl.semaphore_wait(barrier, n - 1)
 
     for p in range(AHEAD):
         if p % SPLIT == 0:
@@ -150,49 +146,21 @@
             out = (out * inv[tile]).astype(jnp.bfloat16)
             o_ref[pl.ds(tile * TILE, TILE), cols] = out
             partial += jnp.sum(out.astype(jnp.float32), axis=0, keepdims=True)
-        sums[b, pl.ds(h, 1), :] = partial
-
-    def step(t, carry):
-        @pl.when(t < pieces)
-        def _():
-            z_copy(t).wait_recv()
-            y_copy(t).start()
-            z_copy(t).wait_send()
-
-            @pl.when(t + AHEAD < pieces)
-            def _():
-                @pl.when(lax.rem(t + AHEAD, SPLIT) == 0)
-                def _():
-                    own_wait(t + AHEAD)
-
-                z_copy(t + AHEAD).start()
-
-        @pl.when((t >= LAG_Y) & (t < pieces + LAG_Y))
-        def _():
-            y_copy(t - LAG_Y).wait_recv()
-            c_near(t - LAG_Y).start()
-            c_far(t - LAG_Y).start()
-
-        @pl.when(t >= LAG_Y + LAG_C)
-        def _():
-            u = t - LAG_Y - LAG_C
-            c_near(u).wait_recv()
-            c_far(u).wait_recv()
-            phase = lax.rem(u, 2 * SPLIT)
-            head = u // (2 * SPLIT)
-            for tile in range(rows // TILE):
-
-                @pl.when(phase == SPLIT - 1)
-                def _():
-                    weigh(head, tile)
-
-            @pl.when(phase == 2 * SPLIT - 1)
-            def _():
-                gather(head)
-
-        return carry
-
-    lax.fori_loop(0, pieces + LAG_Y + LAG_C, step, 0)
+
+        @pl.when(h < HEADS - 1)
+        def _():
+            sums[b, pl.ds(h, 1), :] = partial
+
+        @pl.when(h == HEADS - 2)
+        def _():
+            for k in range(1, PLANE):
+                plane_copy(k).start()
+
+        @pl.when(h == HEADS - 1)
+        def _():
+            lasts[me] = partial
+            for k in range(1, n):
+                last_copy(k).start()
 
     def exchange(buf, slot, peer, stage, index):
         return pltpu.make_async_remote_copy(
@@ -204,11 +172,72 @@
             device_id_type=MESH,
         )
 
-    copies = [
-        exchange(sums, b, base + lax.rem(b + k, PLANE), 0, k) for k in range(1, PLANE)
-    ]
-    for copy in copies:
-        copy.start()
+    def plane_copy(k):
+        return exchange(sums, b, base + lax.rem(b + k, PLANE), 0, k)
+
+    def chain_copy(k):
+        return exchange(planes, a, lax.rem(me + PLANE * k, n), 1, k)
+
+    def last_copy(k):
+        return exchange(lasts, me, lax.rem(me + k, n), 2, k)
+
+    def add_plane():
+        for k in range(1, PLANE):
+            plane_copy(k).wait_send()
+            exchange(sums, lax.rem(b + PLANE - k, PLANE), me, 0, k).wait_recv()
+        plane = sums[0]
+        for k in range(1, PLANE):
+            plane += sums[k]
+        planes[a] = plane
+        for k in range(1, plane_count):
+            chain_copy(k).start()
+
+    def step(t, carry):
+        @pl.when(t < pieces)
+        def _():
+            z_copy(t).wait_recv()
+            y_copy(t).start()
+            z_copy(t).wait_send()
+
+            @pl.when(t + AHEAD < pieces)
+            def _():
+                @pl.when(lax.rem(t + AHEAD, SPLIT) == 0)
+                def _():
+                    own_wait(t + AHEAD)
+
+                z_copy(t + AHEAD).start()
+
+        @pl.when((t >= LAG_Y) & (t < pieces + LAG_Y))
+        def _():
+            y_copy(t - LAG_Y).wait_recv()
+            c_near(t - LAG_Y).start()
+            c_far(t - LAG_Y).start()
+
+        @pl.when(t >= LAG_Y + LAG_C)
+        def _():
+            u = t - LAG_Y - LAG_C
+            c_near(u).wait_recv()
+            c_far(u).wait_recv()
+            phase = lax.rem(u, 2 * SPLIT)
+            head = u // (2 * SPLIT)
+            for tile in range(rows // TILE):
+
+                @pl.when(phase == SPLIT - 1)
+                def _():
+                    weigh(head, tile)
+
+            @pl.when((phase == SPLIT - 1) & (head == HEADS - 1))
+            def _():
+                add_plane()
+
+            @pl.when(phase == 2 * SPLIT - 1)
+            def _():
+                gather(head)
+
+        return carry
+
+    sums[b, pl.ds(HEADS - 1, 1), :] = jnp.zeros((1, HEAD_DIM), jnp.float32)
+    lax.fori_loop(0, pieces + LAG_Y + LAG_C, step, 0)
 
     def drain(h, carry):
         y_copy(h).wait_send()
@@ -217,25 +246,20 @@
         return carry
 
     lax.fori_loop(0, pieces, drain, 0)
-    for k, copy in enumerate(copies, 1):
-        copy.wait_send()
-        exchange(sums, lax.rem(b + PLANE - k, PLANE), me, 0, k).wait_recv()
-    plane = sums[0]
-    for k in range(1, PLANE):
-        plane += sums[k]
-    planes[a] = plane
-    copies = [
-        exchange(planes, a, lax.rem(me + PLANE * k, n), 1, k) for k in range(1, plane_count)
-    ]
-    for copy in copies:
-        copy.start()
-    for k, copy in enumerate(copies, 1):
-        copy.wait_send()
+    for k in range(1, plane_count):
+        chain_copy(k).wait_send()
         exchange(planes, lax.rem(a + plane_count - k, plane_count), me, 1, k).wait_recv()
     total = planes[0]
     for k in range(1, plane_count):
         total += planes[k]
     prof_ref[...] = total / math.sqrt(rows * n)
+    for k in range(1, n):
+        last_copy(k).wait_send()
+        exchange(lasts, lax.rem(me + n - k, n), me, 2, k).wait_recv()
+    last = lasts[0]
+    for k in range(1, n):
+        last += lasts[k]
+    prof_ref[pl.ds(HEADS - 1, 1), :] = last / math.sqrt(rows * n)
 
 
 def body(n, queries, key_rows, values):
@@ -244,7 +268,6 @@
     if rows * PLANE != WINDOW or n % PLANE or plane_count < 2:
         raise ValueError("unsupported sizes")
     pieces = 2 * HEADS * SPLIT
-    stages = max(PLANE, plane_count)
     hbm_spec = pl.BlockSpec(memory_space=pltpu.HBM)
     vmem_spec = pl.BlockSpec(memory_space=pltpu.VMEM)
     dma = pltpu.SemaphoreType.DMA
@@ -263,14 +286,15 @@
             pltpu.VMEM((rows // TILE, TILE, 1), jnp.float32),
             pltpu.VMEM((PLANE, HEADS, HEAD_DIM), jnp.float32),
             pltpu.VMEM((plane_count, HEADS, HEAD_DIM), jnp.float32),
+            pltpu.VMEM((n, 1, HEAD_DIM), jnp.float32),
             dma,
             dma((2 * HEADS,)),
             dma((pieces,)),
             dma((pieces,)),
             dma((2, pieces)),
             dma((PLANE, pieces)),
-            dma((2, stages)),
-            dma((2, stages)),
+            dma((3, n)),
+            dma((3, n)),
         ],
         compiler_params=pltpu.CompilerParams(
             collective_id=0, has_side_effects=True, vmem_limit_bytes=51 * 1024 * 1024

time: 115 us -> 114 us (level)
  no operation moved by 1% of the time
where the time goes in v3:
time: 114 us
  Pallas kernels  111 us (97%)
  local copies, waits for them, and re-layouts  1.92 us (2%)
    pallas_call x1, Pallas kernels, body(): pl.pallas_call(functools.partial(kernel, n), out_shape=(jax.ShapeDtypeStr...  111 us

profile of v3, /device:TPU:0, one launch (start us, length us, event | category | flops | bytes accessed | tf_op | source)
XLA Modules:
  0.0 113.9 jit_solution(1680853789255771766)
XLA Ops:
  0.6 111.3 %ring_attention.1 = (bf16[512,2048]{1,0:T(8,128)(2,1)S(1)}, f32[16,128]{1,0:T(8,128)S(1)}) custom-call(bf16[512,2048]{1,0:T(8,128)(2,1)} %q_ref.1, bf16[512,2048]{1,0:T(8,128)(2,1)} %k_ref.1, bf16[512,2048]{1,0:T(8,128)(2,1)} %v_ref.1), custom_call_target="tpu_custom_call" | custom-call | tf_op jit(solution)/shard_map/ring_attention/pallas_call | solution.py:274
  111.9 1.3 %copy.7 = bf16[512,2048]{1,0:T(8,128)(2,1)} copy(bf16[512,2048]{1,0:T(8,128)(2,1)S(1)} %get-tuple-element.8) | data formatting | bytes 4194304
  113.3 0.6 copy.8
